TPU v7x, 32 devices: a whole 2x2x4 slice. The times are simulated.
32 devices in a mesh: member: 8 (over z, x), space: 4 (over y, core).
Axes of the slice: x: 2, y: 2, z: 4, core: 2. Of those that a mesh axis runs over, the one named last changes fastest.
Arguments:
- alpha: float32 [16, 16, 32, 1280], P('member', None, 'space'), may hold values from -6 to 6
- perturb: bfloat16 [4, 16, 16, 32, 1280], P(None, 'member', None, 'space'), may hold values from -1.5 to 1.5
- kappa: float32 [32, 1280], P('space'), may hold values from 0.1 to 0.24
- land: int32 [32, 1280], P('space'), may hold values 0 or 1
- obs_weight: float32 [4, 16, 32, 1280], P(None, 'member', 'space'), may hold values from 0.2 to 5
- innovation: float32 [4, 16, 32, 1280], P(None, 'member', 'space'), may hold values from -6 to 6
Outputs:
- gradient: float32 [16, 16, 32, 1280], P('member', None, 'space')
- weighted_misfit: float32 [4, 16, 32, 1280], P(None, 'member', 'space')
All inputs are finite; a program needn't handle non-finite values. No bound on the sum of `land` on one device may be relied on, other than what follows from the above.
Results may differ from a plain program's by a relative error of at most 0.0003.
Values sent between devices are 32-bit elements; how exact they have to be, the bound alone decides.
No kernel may reach another device: no remote copies, remote signals or barrier semaphores. Data moves between devices by JAX's collectives and lax.ppermute only.
A program may use at most 64 MiB of HBM per device.

v0:
```python
import jax
import jax.numpy as jnp
from jax import lax
from jax.sharding import PartitionSpec as P

STEPS = 4


def extended_2(cells, sides, width):
    for axis, dim in sides:
        count = lax.axis_size(axis)
        ends = count - 1
        head = lax.slice_in_dim(cells, 0, width, axis=dim)
        tail = lax.slice_in_dim(cells, cells.shape[dim] - width, cells.shape[dim], axis=dim)
        cells = jnp.concatenate(
            [
                lax.ppermute(tail, axis, [(i, (i + 1) % count) for i in range(ends)]),
                cells,
                lax.ppermute(head, axis, [((i + 1) % count, i) for i in range(ends)]),
            ],
            axis=dim,
        )
    return cells


def smooth_step(padded, coef_east, coef_west, coef_north, coef_south):
    middle = padded[:, :, 1:-1, :]
    return (
        middle
        + coef_east * (jnp.roll(middle, -1, axis=-1) - middle)
        + coef_west * (jnp.roll(middle, 1, axis=-1) - middle)
        + coef_north * (padded[:, :, 2:, :] - middle)
        + coef_south * (padded[:, :, :-2, :] - middle)
    )


def body(alpha, perturb, kappa, land, obs_weight, innovation):
    tile_rows = alpha.shape[2]
    extended = extended_2(kappa, (("space", 0),), STEPS + 1)
    inner = extended[1:-1]
    coef_north = 0.5 * (inner + extended[2:])
    coef_south = 0.5 * (inner + extended[:-2])
    coef_east = 0.5 * (inner + jnp.roll(inner, -1, axis=1))
    coef_west = 0.5 * (inner + jnp.roll(inner, 1, axis=1))

    def diffuse(field):
        current = field
        for sweep in range(STEPS):
            padded = extended_2(current, (("space", 2),), 1)
            current = smooth_step(
                padded,
                coef_east[STEPS : STEPS + tile_rows],
                coef_west[STEPS : STEPS + tile_rows],
                coef_north[STEPS : STEPS + tile_rows],
                coef_south[STEPS : STEPS + tile_rows],
            )
        return current

    sea = land.astype(jnp.float32)
    local = diffuse(alpha) * sea
    partial_sum = jnp.sum(perturb * local[None], axis=1)
    total = lax.psum(partial_sum, "member")
    weight_all, innov_all = (
        lax.all_gather(obs_weight, "member", axis=1, tiled=True),
        lax.all_gather(innovation, "member", axis=1, tiled=True),
    )
    whole_misfit = weight_all * (total - innov_all)
    own_width = obs_weight.shape[1]
    weighted_misfit = lax.dynamic_slice_in_dim(
        whole_misfit, lax.axis_index("member") * own_width, own_width, 1
    )
    back = jnp.sum(perturb * whole_misfit[:, None], axis=0)
    gradient = diffuse(back * sea) + alpha
    return (gradient, weighted_misfit)


def solution(mesh):
    placed = (
        P("member", None, "space", None),
        P(None, "member", None, "space", None),
        P("space", None),
        P("space", None),
        P(None, "member", "space", None),
        P(None, "member", "space", None),
    )
    return jax.shard_map(
        body,
        mesh=mesh,
        in_specs=placed,
        out_specs=(P("member", None, "space", None), P(None, "member", "space", None)),
        check_vma=False,
    )
```

profile of v0, /device:TPU:1, one launch (start us, length us, event | category | flops | bytes accessed | tf_op | source)
XLA Modules:
  0.0 342.5 jit_solution(4764403704498449764)
XLA Ops:
  7.2 0.9 fusion.116
  8.1 4.5 %collective-permute-start = (f32[5,1280]{1,0:T(8,128)S(1)}, f32[5,1280]{1,0:T(8,128)S(1)}, u32[]{:S(2)}, u32[]{:S(2)}) collective-permute-start(f32[5,1280]{1,0:T(8,128)S(1)} %get-tuple-element.61), channel_id=1, source_target_pairs={{0,1},{1,2},{2,3},{4,5},{5,6},{6,7},{8,9},{9,10},{10,11},{12,13},{... | collective-permute-start | bytes 76808 | tf_op jit(solution)/shard_map/ppermute | solution.py:17
  12.6 1.9 collective-permute-start.1
  14.6 2.1 fusion.113
  16.7 1.9 collective-permute-start.2
  18.7 3.8 %collective-permute-start.3 = (f32[2,16,1,1280]{3,1,2,0:T(8,128)S(1)}, f32[2,16,1,1280]{3,1,2,0:T(8,128)S(1)}, u32[]{:S(2)}, u32[]{:S(2)}) collective-permute-start(f32[2,16,1,1280]{3,1,2,0:T(8,128)S(1)} %copy.57), channel_id=1, source_target_pairs={{0,1},{1,2},{2,3},{4,5},{5,6},{6,7},{8,9},{9,10},{10,11},{12,13},{... | collective-permute-start | bytes 491528 | tf_op jit(solution)/shard_map/ppermute | solution.py:17
  22.4 0.4 fusion.112
  23.5 1.2 collective-permute-done.3
  24.9 1.0 fusion.48
  25.9 0.4 fusion.109
  26.3 0.2 fusion.110
  26.5 1.9 collective-permute-start.4
  28.5 4.4 %collective-permute-start.5 = (f32[2,16,1,1280]{3,1,2,0:T(8,128)S(1)}, f32[2,16,1,1280]{3,1,2,0:T(8,128)S(1)}, u32[]{:S(2)}, u32[]{:S(2)}) collective-permute-start(f32[2,16,1,1280]{3,1,2,0:T(8,128)S(1)} %copy.30), channel_id=1, source_target_pairs={{0,1},{1,2},{2,3},{4,5},{5,6},{6,7},{8,9},{9,10},{10,11},{12,13},{... | collective-permute-start | bytes 491528 | tf_op jit(solution)/shard_map/ppermute | solution.py:17
  33.0 0.9 collective-permute-done.4
  34.1 1.0 collective-permute-done.5
  35.3 1.0 fusion.42
  36.3 0.4 fusion.106
  36.8 0.2 fusion.107
  37.0 1.9 collective-permute-start.6
  38.9 4.4 %collective-permute-start.7 = (f32[2,16,1,1280]{3,1,2,0:T(8,128)S(1)}, f32[2,16,1,1280]{3,1,2,0:T(8,128)S(1)}, u32[]{:S(2)}, u32[]{:S(2)}) collective-permute-start(f32[2,16,1,1280]{3,1,2,0:T(8,128)S(1)} %copy.34), channel_id=1, source_target_pairs={{0,1},{1,2},{2,3},{4,5},{5,6},{6,7},{8,9},{9,10},{10,11},{12,13},{... | collective-permute-start | bytes 491528 | tf_op jit(solution)/shard_map/ppermute | solution.py:17
  43.4 0.9 collective-permute-done.6
  44.5 1.0 collective-permute-done.7
  45.7 1.0 fusion.36
  46.8 0.4 fusion.103
  47.2 0.2 fusion.104
  47.4 1.9 collective-permute-start.8
  49.4 4.4 %collective-permute-start.9 = (f32[2,16,1,1280]{3,1,2,0:T(8,128)S(1)}, f32[2,16,1,1280]{3,1,2,0:T(8,128)S(1)}, u32[]{:S(2)}, u32[]{:S(2)}) collective-permute-start(f32[2,16,1,1280]{3,1,2,0:T(8,128)S(1)} %copy.38), channel_id=1, source_target_pairs={{0,1},{1,2},{2,3},{4,5},{5,6},{6,7},{8,9},{9,10},{10,11},{12,13},{... | collective-permute-start | bytes 491528 | tf_op jit(solution)/shard_map/ppermute | solution.py:17
  53.9 0.9 collective-permute-done.8
  55.0 1.0 collective-permute-done.9
  56.2 1.1 fusion.30
  57.3 0.7 copy-done.1
  57.9 2.1 fusion
  60.1 0.7 all-gather.3.cloned.1.call-update
  60.9 0.2 all-gather.5.cloned.1.call-start
  61.1 0.5 all-gather.5.cloned.1.call-update
  61.6 115.5 %all-reduce.2.cloned.1.call-done = f32[4,16,8,1280]{3,2,1,0:T(8,128)} async-done(((f32[4,16,8,1280]{3,2,1,0:T(8,128)}), f32[4,16,8,1280]{3,2,1,0:T(8,128)}) %all-reduce.2.cloned.1.call-update) | async-done | bytes 2621456 | tf_op jit(solution)/shard_map/psum | solution.py:62
  177.0 55.2 %all-gather.3.cloned.1.call-done = f32[4,16,8,1280]{3,2,1,0:T(8,128)} async-done(((f32[4,2,8,1280]{3,2,1,0:T(8,128)}), f32[4,16,8,1280]{3,2,1,0:T(8,128)}) %all-gather.3.cloned.1.call-update) | async-done | bytes 2621456 | tf_op jit(solution)/shard_map/all_gather | solution.py:64
  232.2 55.2 %all-gather.5.cloned.1.call-done = f32[4,16,8,1280]{3,2,1,0:T(8,128)} async-done(((f32[4,2,8,1280]{3,2,1,0:T(8,128)}), f32[4,16,8,1280]{3,2,1,0:T(8,128)}) %all-gather.5.cloned.1.call-update) | async-done | bytes 2621456 | tf_op jit(solution)/shard_map/all_gather | solution.py:65
  287.5 3.9 %subtract_multiply_fusion = f32[4,16,8,1280]{3,2,1,0:T(8,128)S(1)} fusion(f32[4,16,8,1280]{3,2,1,0:T(8,128)} %all-gather.3.cloned.1.call-done, f32[4,16,8,1280]{3,2,1,0:T(8,128)} %all-reduce.2.cloned.1.call-done, f32[4,16,8,1280]{3,2,1,0:T(8,128)} %all-gather.5.cloned.1.call-done), kind=kLoop, calls=%fused_computation.4 | loop fusion | flops 1310720 | bytes 10485760 | tf_op jit(solution)/shard_map/mul | solution.py:67
  291.5 0.6 fusion.1
  292.2 0.4 fusion.100
  292.8 4.2 %collective-permute-start.10 = (f32[2,16,1,1280]{3,1,2,0:T(8,128)S(1)}, f32[2,16,1,1280]{3,1,2,0:T(8,128)S(1)}, u32[]{:S(2)}, u32[]{:S(2)}) collective-permute-start(f32[2,16,1,1280]{3,1,2,0:T(8,128)S(1)} %copy.40), channel_id=1, source_target_pairs={{1,0},{2,1},{3,2},{5,4},{6,5},{7,6},{9,8},{10,9},{11,10},{13,12},{... | collective-permute-start | bytes 491528 | tf_op jit(solution)/shard_map/ppermute | solution.py:19
  297.0 3.0 collective-permute-start.11
  300.0 0.8 constant_dynamic-slice_fusion
  301.3 1.0 collective-permute-done.11
  302.5 1.0 fusion.23
  303.5 0.4 fusion.97
  304.1 1.9 collective-permute-start.12
  306.1 4.4 %collective-permute-start.13 = (f32[2,16,1,1280]{3,1,2,0:T(8,128)S(1)}, f32[2,16,1,1280]{3,1,2,0:T(8,128)S(1)}, u32[]{:S(2)}, u32[]{:S(2)}) collective-permute-start(f32[2,16,1,1280]{3,1,2,0:T(8,128)S(1)} %copy.46), channel_id=1, source_target_pairs={{0,1},{1,2},{2,3},{4,5},{5,6},{6,7},{8,9},{9,10},{10,11},{12,13},{... | collective-permute-start | bytes 491528 | tf_op jit(solution)/shard_map/ppermute | solution.py:17
  310.6 0.9 collective-permute-done.12
  311.7 1.0 collective-permute-done.13
  312.9 1.0 fusion.17
  313.9 0.4 fusion.94
  314.6 1.9 collective-permute-start.14
  316.5 4.4 %collective-permute-start.15 = (f32[2,16,1,1280]{3,1,2,0:T(8,128)S(1)}, f32[2,16,1,1280]{3,1,2,0:T(8,128)S(1)}, u32[]{:S(2)}, u32[]{:S(2)}) collective-permute-start(f32[2,16,1,1280]{3,1,2,0:T(8,128)S(1)} %copy.50), channel_id=1, source_target_pairs={{0,1},{1,2},{2,3},{4,5},{5,6},{6,7},{8,9},{9,10},{10,11},{12,13},{... | collective-permute-start | bytes 491528 | tf_op jit(solution)/shard_map/ppermute | solution.py:17
  321.0 0.9 collective-permute-done.14
  322.1 1.0 collective-permute-done.15
  323.3 1.1 fusion.11
  324.4 0.4 fusion.91
  325.1 1.9 collective-permute-start.16
  327.0 4.4 %collective-permute-start.17 = (f32[2,16,1,1280]{3,1,2,0:T(8,128)S(1)}, f32[2,16,1,1280]{3,1,2,0:T(8,128)S(1)}, u32[]{:S(2)}, u32[]{:S(2)}) collective-permute-start(f32[2,16,1,1280]{3,1,2,0:T(8,128)S(1)} %copy.54), channel_id=1, source_target_pairs={{0,1},{1,2},{2,3},{4,5},{5,6},{6,7},{8,9},{9,10},{10,11},{12,13},{... | collective-permute-start | bytes 491528 | tf_op jit(solution)/shard_map/ppermute | solution.py:17
  331.5 0.9 collective-permute-done.16
  332.6 1.0 collective-permute-done.17
  333.8 2.2 fusion.5
  (66 shorter events, 5.2 us)
Async XLA Ops:
  7.2 15.3 %copy-start = (f32[2,16,8,1280]{3,2,1,0:T(8,128)S(1)}, f32[2,16,8,1280]{3,2,1,0:T(8,128)}, u32[]{:S(2)}) copy-start(f32[2,16,8,1280]{3,2,1,0:T(8,128)} %param.6) | copy-start | bytes 3932164
  7.2 169.9 %all-reduce.2.cloned.1.call-start = ((), (), s32[]{:S(2)}) async-start(), calls=%async_computation.1 | async-start | bytes 5242880 | tf_op jit(solution)/shard_map/psum | solution.py:62
  8.1 14.9 %collective-permute-start = (f32[5,1280]{1,0:T(8,128)S(1)}, f32[5,1280]{1,0:T(8,128)S(1)}, u32[]{:S(2)}, u32[]{:S(2)}) collective-permute-start(f32[5,1280]{1,0:T(8,128)S(1)} %get-tuple-element.61), channel_id=1, source_target_pairs={{0,1},{1,2},{2,3},{4,5},{5,6},{6,7},{8,9},{9,10},{10,11},{12,13},{... | collective-permute-start | bytes 76808 | tf_op jit(solution)/shard_map/ppermute | solution.py:17
  12.6 10.4 %collective-permute-start.1 = (f32[5,1280]{1,0:T(8,128)S(1)}, f32[5,1280]{1,0:T(8,128)S(1)}, u32[]{:S(2)}, u32[]{:S(2)}) collective-permute-start(f32[5,1280]{1,0:T(8,128)S(1)} %get-tuple-element.62), channel_id=1, source_target_pairs={{1,0},{2,1},{3,2},{5,4},{6,5},{7,6},{9,8},{10,9},{11,10},{13,12},{... | collective-permute-start | bytes 76808 | tf_op jit(solution)/shard_map/ppermute | solution.py:19
  16.7 6.6 %collective-permute-start.2 = (f32[2,16,1,1280]{3,1,2,0:T(8,128)S(1)}, f32[2,16,1,1280]{3,1,2,0:T(8,128)S(1)}, u32[]{:S(2)}, u32[]{:S(2)}) collective-permute-start(f32[2,16,1,1280]{3,1,2,0:T(8,128)S(1)} %copy.56), channel_id=1, source_target_pairs={{1,0},{2,1},{3,2},{5,4},{6,5},{7,6},{9,8},{10,9},{11,10},{13,12},{... | collective-permute-start | bytes 491528 | tf_op jit(solution)/shard_map/ppermute | solution.py:19
  18.6 4.3 %copy-start.4 = (s32[8,1280]{1,0:T(8,128)S(1)}, s32[8,1280]{1,0:T(8,128)}, u32[]{:S(2)}) copy-start(s32[8,1280]{1,0:T(8,128)} %param.9) | copy-start | bytes 122884
  18.6 4.4 %copy-start.3 = (f32[8,1280]{1,0:T(8,128)S(1)}, f32[8,1280]{1,0:T(8,128)}, u32[]{:S(2)}) copy-start(f32[8,1280]{1,0:T(8,128)} %param.8) | copy-start | bytes 122884
  18.7 6.0 %collective-permute-start.3 = (f32[2,16,1,1280]{3,1,2,0:T(8,128)S(1)}, f32[2,16,1,1280]{3,1,2,0:T(8,128)S(1)}, u32[]{:S(2)}, u32[]{:S(2)}) collective-permute-start(f32[2,16,1,1280]{3,1,2,0:T(8,128)S(1)} %copy.57), channel_id=1, source_target_pairs={{0,1},{1,2},{2,3},{4,5},{5,6},{6,7},{8,9},{9,10},{10,11},{12,13},{... | collective-permute-start | bytes 491528 | tf_op jit(solution)/shard_map/ppermute | solution.py:17
  26.5 7.4 %collective-permute-start.4 = (f32[2,16,1,1280]{3,1,2,0:T(8,128)S(1)}, f32[2,16,1,1280]{3,1,2,0:T(8,128)S(1)}, u32[]{:S(2)}, u32[]{:S(2)}) collective-permute-start(f32[2,16,1,1280]{3,1,2,0:T(8,128)S(1)} %copy.28), channel_id=1, source_target_pairs={{1,0},{2,1},{3,2},{5,4},{6,5},{7,6},{9,8},{10,9},{11,10},{13,12},{... | collective-permute-start | bytes 491528 | tf_op jit(solution)/shard_map/ppermute | solution.py:19
  28.5 6.6 %collective-permute-start.5 = (f32[2,16,1,1280]{3,1,2,0:T(8,128)S(1)}, f32[2,16,1,1280]{3,1,2,0:T(8,128)S(1)}, u32[]{:S(2)}, u32[]{:S(2)}) collective-permute-start(f32[2,16,1,1280]{3,1,2,0:T(8,128)S(1)} %copy.30), channel_id=1, source_target_pairs={{0,1},{1,2},{2,3},{4,5},{5,6},{6,7},{8,9},{9,10},{10,11},{12,13},{... | collective-permute-start | bytes 491528 | tf_op jit(solution)/shard_map/ppermute | solution.py:17
  37.0 7.4 %collective-permute-start.6 = (f32[2,16,1,1280]{3,1,2,0:T(8,128)S(1)}, f32[2,16,1,1280]{3,1,2,0:T(8,128)S(1)}, u32[]{:S(2)}, u32[]{:S(2)}) collective-permute-start(f32[2,16,1,1280]{3,1,2,0:T(8,128)S(1)} %copy.32), channel_id=1, source_target_pairs={{1,0},{2,1},{3,2},{5,4},{6,5},{7,6},{9,8},{10,9},{11,10},{13,12},{... | collective-permute-start | bytes 491528 | tf_op jit(solution)/shard_map/ppermute | solution.py:19
  38.9 6.6 %collective-permute-start.7 = (f32[2,16,1,1280]{3,1,2,0:T(8,128)S(1)}, f32[2,16,1,1280]{3,1,2,0:T(8,128)S(1)}, u32[]{:S(2)}, u32[]{:S(2)}) collective-permute-start(f32[2,16,1,1280]{3,1,2,0:T(8,128)S(1)} %copy.34), channel_id=1, source_target_pairs={{0,1},{1,2},{2,3},{4,5},{5,6},{6,7},{8,9},{9,10},{10,11},{12,13},{... | collective-permute-start | bytes 491528 | tf_op jit(solution)/shard_map/ppermute | solution.py:17
  47.4 7.4 %collective-permute-start.8 = (f32[2,16,1,1280]{3,1,2,0:T(8,128)S(1)}, f32[2,16,1,1280]{3,1,2,0:T(8,128)S(1)}, u32[]{:S(2)}, u32[]{:S(2)}) collective-permute-start(f32[2,16,1,1280]{3,1,2,0:T(8,128)S(1)} %copy.36), channel_id=1, source_target_pairs={{1,0},{2,1},{3,2},{5,4},{6,5},{7,6},{9,8},{10,9},{11,10},{13,12},{... | collective-permute-start | bytes 491528 | tf_op jit(solution)/shard_map/ppermute | solution.py:19
  49.4 6.6 %collective-permute-start.9 = (f32[2,16,1,1280]{3,1,2,0:T(8,128)S(1)}, f32[2,16,1,1280]{3,1,2,0:T(8,128)S(1)}, u32[]{:S(2)}, u32[]{:S(2)}) collective-permute-start(f32[2,16,1,1280]{3,1,2,0:T(8,128)S(1)} %copy.38), channel_id=1, source_target_pairs={{0,1},{1,2},{2,3},{4,5},{5,6},{6,7},{8,9},{9,10},{10,11},{12,13},{... | collective-permute-start | bytes 491528 | tf_op jit(solution)/shard_map/ppermute | solution.py:17
  56.2 1.7 copy-start.1
  60.1 172.1 %all-gather.3.cloned.1.call-start = ((), (), s32[]{:S(2)}) async-start(), calls=%async_computation | async-start | bytes 2949120 | tf_op jit(solution)/shard_map/all_gather | solution.py:64
  60.9 226.6 %all-gather.5.cloned.1.call-start = ((), (), s32[]{:S(2)}) async-start(), calls=%async_computation.2 | async-start | bytes 2949120 | tf_op jit(solution)/shard_map/all_gather | solution.py:65
  287.5 4.0 %copy-start.2 = (bf16[4,2,16,8,1280]{4,3,2,1,0:T(8,128)(2,1)S(1)}, bf16[4,2,16,8,1280]{4,3,2,1,0:T(8,128)(2,1)}, u32[]{:S(2)}) copy-start(bf16[4,2,16,8,1280]{4,3,2,1,0:T(8,128)(2,1)} %param.7) | copy-start | bytes 7864324
  292.8 8.2 %collective-permute-start.10 = (f32[2,16,1,1280]{3,1,2,0:T(8,128)S(1)}, f32[2,16,1,1280]{3,1,2,0:T(8,128)S(1)}, u32[]{:S(2)}, u32[]{:S(2)}) collective-permute-start(f32[2,16,1,1280]{3,1,2,0:T(8,128)S(1)} %copy.40), channel_id=1, source_target_pairs={{1,0},{2,1},{3,2},{5,4},{6,5},{7,6},{9,8},{10,9},{11,10},{13,12},{... | collective-permute-start | bytes 491528 | tf_op jit(solution)/shard_map/ppermute | solution.py:19
  297.0 5.2 %collective-permute-start.11 = (f32[2,16,1,1280]{3,1,2,0:T(8,128)S(1)}, f32[2,16,1,1280]{3,1,2,0:T(8,128)S(1)}, u32[]{:S(2)}, u32[]{:S(2)}) collective-permute-start(f32[2,16,1,1280]{3,1,2,0:T(8,128)S(1)} %copy.42), channel_id=1, source_target_pairs={{0,1},{1,2},{2,3},{4,5},{5,6},{6,7},{8,9},{9,10},{10,11},{12,13},{... | collective-permute-start | bytes 491528 | tf_op jit(solution)/shard_map/ppermute | solution.py:17
  304.1 7.4 %collective-permute-start.12 = (f32[2,16,1,1280]{3,1,2,0:T(8,128)S(1)}, f32[2,16,1,1280]{3,1,2,0:T(8,128)S(1)}, u32[]{:S(2)}, u32[]{:S(2)}) collective-permute-start(f32[2,16,1,1280]{3,1,2,0:T(8,128)S(1)} %copy.44), channel_id=1, source_target_pairs={{1,0},{2,1},{3,2},{5,4},{6,5},{7,6},{9,8},{10,9},{11,10},{13,12},{... | collective-permute-start | bytes 491528 | tf_op jit(solution)/shard_map/ppermute | solution.py:19
  306.1 6.6 %collective-permute-start.13 = (f32[2,16,1,1280]{3,1,2,0:T(8,128)S(1)}, f32[2,16,1,1280]{3,1,2,0:T(8,128)S(1)}, u32[]{:S(2)}, u32[]{:S(2)}) collective-permute-start(f32[2,16,1,1280]{3,1,2,0:T(8,128)S(1)} %copy.46), channel_id=1, source_target_pairs={{0,1},{1,2},{2,3},{4,5},{5,6},{6,7},{8,9},{9,10},{10,11},{12,13},{... | collective-permute-start | bytes 491528 | tf_op jit(solution)/shard_map/ppermute | solution.py:17
  314.6 7.4 %collective-permute-start.14 = (f32[2,16,1,1280]{3,1,2,0:T(8,128)S(1)}, f32[2,16,1,1280]{3,1,2,0:T(8,128)S(1)}, u32[]{:S(2)}, u32[]{:S(2)}) collective-permute-start(f32[2,16,1,1280]{3,1,2,0:T(8,128)S(1)} %copy.48), channel_id=1, source_target_pairs={{1,0},{2,1},{3,2},{5,4},{6,5},{7,6},{9,8},{10,9},{11,10},{13,12},{... | collective-permute-start | bytes 491528 | tf_op jit(solution)/shard_map/ppermute | solution.py:19
  316.5 6.6 %collective-permute-start.15 = (f32[2,16,1,1280]{3,1,2,0:T(8,128)S(1)}, f32[2,16,1,1280]{3,1,2,0:T(8,128)S(1)}, u32[]{:S(2)}, u32[]{:S(2)}) collective-permute-start(f32[2,16,1,1280]{3,1,2,0:T(8,128)S(1)} %copy.50), channel_id=1, source_target_pairs={{0,1},{1,2},{2,3},{4,5},{5,6},{6,7},{8,9},{9,10},{10,11},{12,13},{... | collective-permute-start | bytes 491528 | tf_op jit(solution)/shard_map/ppermute | solution.py:17
  325.1 7.4 %collective-permute-start.16 = (f32[2,16,1,1280]{3,1,2,0:T(8,128)S(1)}, f32[2,16,1,1280]{3,1,2,0:T(8,128)S(1)}, u32[]{:S(2)}, u32[]{:S(2)}) collective-permute-start(f32[2,16,1,1280]{3,1,2,0:T(8,128)S(1)} %copy.52), channel_id=1, source_target_pairs={{1,0},{2,1},{3,2},{5,4},{6,5},{7,6},{9,8},{10,9},{11,10},{13,12},{... | collective-permute-start | bytes 491528 | tf_op jit(solution)/shard_map/ppermute | solution.py:19
  327.0 6.6 %collective-permute-start.17 = (f32[2,16,1,1280]{3,1,2,0:T(8,128)S(1)}, f32[2,16,1,1280]{3,1,2,0:T(8,128)S(1)}, u32[]{:S(2)}, u32[]{:S(2)}) collective-permute-start(f32[2,16,1,1280]{3,1,2,0:T(8,128)S(1)} %copy.54), channel_id=1, source_target_pairs={{0,1},{1,2},{2,3},{4,5},{5,6},{6,7},{8,9},{9,10},{10,11},{12,13},{... | collective-permute-start | bytes 491528 | tf_op jit(solution)/shard_map/ppermute | solution.py:17
Sparse Core Ops, SparseCore 0:
  60.2 116.7 all-reduce.1
  179.2 52.9 all-gather.2
  234.4 52.9 all-gather.4
where the time goes:
time: 343 us
  waiting for transfers between devices  241 us (70%)
  starting transfers between devices  57.5 us (17%)
  other arithmetic  16.3 us (5%)
  between operations  14.4 us (4%)
  local copies, waits for them, and re-layouts  13.1 us (4%)
    psum x1, waiting for transfers between devices, body(): total = lax.psum(partial_sum, 'member')  115 us
    all_gather x1, waiting for transfers between devices, body(): lax.all_gather(innovation, 'member', axis=1, tiled=True)  55.2 us
    all_gather x1, waiting for transfers between devices, body(): lax.all_gather(obs_weight, 'member', axis=1, tiled=True)  55.2 us
    ppermute x9, starting transfers between devices, extended_2(): lax.ppermute(tail, axis, [(i, (i + 1) % count) for i in range(ends)])  37.6 us
    ppermute x9, starting transfers between devices, extended_2(): lax.ppermute(head, axis, [((i + 1) % count, i) for i in range(ends)])  19.5 us
    ppermute x9, waiting for transfers between devices, extended_2(): lax.ppermute(tail, axis, [(i, (i + 1) % count) for i in range(ends)])  8.39 us
  transfers between devices with their start and end apart: 21, of which 19 were waited for; matrix products, arithmetic and copies ran while one was open for 2% of the time, Pallas kernels for 0%

commit v1 on v0

--- a/solution.py
+++ b/solution.py
@@ -59,7 +59,9 @@
     sea = land.astype(jnp.float32)
     local = diffuse(alpha) * sea
     partial_sum = jnp.sum(perturb * local[None], axis=1)
-    total = lax.psum(partial_sum, "member")
+    total = partial_sum
+    for hop in (1, 2, 4):
+        total = total + lax.ppermute(total, "member", [(dev, dev ^ hop) for dev in range(8)])
     weight_all, innov_all = (
         lax.all_gather(obs_weight, "member", axis=1, tiled=True),
         lax.all_gather(innovation, "member", axis=1, tiled=True),

time: 343 us -> 390 us (1.14)
  waiting for transfers between devices: 241 us -> 279 us
  other arithmetic: 16.3 us -> 22 us
    ppermute x0 -> x3, waiting for transfers between devices: none -> 265 us  [body(): lax.ppermute(total, 'member', [(dev, dev ^ hop) for dev in range(8)])]
    psum x1 -> x0, waiting for transfers between devices: 115 us -> none  [body(): total = lax.psum(partial_sum, 'member')]
    all_gather x1, waiting for transfers between devices: 55.2 us -> 0.01 us  [body(): lax.all_gather(innovation, 'member', axis=1, tiled=True)]
    all_gather x1, waiting for transfers between devices: 55.2 us -> 0.01 us  [body(): lax.all_gather(obs_weight, 'member', axis=1, tiled=True)]
    add x0 -> x2, other arithmetic: none -> 6.33 us  [body(): total + lax.ppermute(total, 'member', [(dev, dev ^ hop) for dev in range(...]
    ppermute x0 -> x3, starting transfers between devices: none -> 4.59 us  [body(): lax.ppermute(total, 'member', [(dev, dev ^ hop) for dev in range(8)])]
  transfers between devices with their start and end apart: 21 -> 23, of which waited for: 19 -> 18; matrix products, arithmetic and copies ran while one was open for 2% -> 5% of each run, Pallas kernels for 0% -> 0%
where the time goes in v1:
time: 390 us; the launch traced here: 389 us
  waiting for transfers between devices  279 us (72%)
  starting transfers between devices  60.5 us (16%)
  other arithmetic  22 us (6%)
  between operations  14.7 us (4%)
  local copies, waits for them, and re-layouts  13 us (3%)
    ppermute x3, waiting for transfers between devices, body(): lax.ppermute(total, 'member', [(dev, dev ^ hop) for dev in range(8)])  265 us
    ppermute x9, starting transfers between devices, extended_2(): lax.ppermute(tail, axis, [(i, (i + 1) % count) for i in range(ends)])  37.1 us
    ppermute x9, starting transfers between devices, extended_2(): lax.ppermute(head, axis, [((i + 1) % count, i) for i in range(ends)])  18.7 us
  transfers between devices with their start and end apart: 23, of which 18 were waited for; matrix products, arithmetic and copies ran while one was open for 5% of the time, Pallas kernels for 0%

profile of v1, /device:TPU:1, one launch (start us, length us, event | category | flops | bytes accessed | tf_op | source)
XLA Modules:
  0.0 389.2 jit_solution(5337938806963436188)
XLA Ops:
  7.2 0.9 fusion.116
  8.1 4.5 %collective-permute-start = (f32[5,1280]{1,0:T(8,128)S(1)}, f32[5,1280]{1,0:T(8,128)S(1)}, u32[]{:S(2)}, u32[]{:S(2)}) collective-permute-start(f32[5,1280]{1,0:T(8,128)S(1)} %get-tuple-element.61), channel_id=1, source_target_pairs={{0,1},{1,2},{2,3},{4,5},{5,6},{6,7},{8,9},{9,10},{10,11},{12,13},{... | collective-permute-start | bytes 76808 | tf_op jit(solution)/shard_map/ppermute | solution.py:17
  12.6 1.9 collective-permute-start.1
  14.6 2.0 fusion.113
  16.6 1.9 collective-permute-start.2
  18.6 3.6 collective-permute-start.3
  22.3 0.4 fusion.112
  23.5 1.0 collective-permute-done.3
  24.6 1.0 fusion.48
  25.6 0.4 fusion.109
  26.3 1.9 collective-permute-start.4
  28.3 4.4 %collective-permute-start.5 = (f32[2,16,1,1280]{3,1,2,0:T(8,128)S(1)}, f32[2,16,1,1280]{3,1,2,0:T(8,128)S(1)}, u32[]{:S(2)}, u32[]{:S(2)}) collective-permute-start(f32[2,16,1,1280]{3,1,2,0:T(8,128)S(1)} %copy.30), channel_id=1, source_target_pairs={{0,1},{1,2},{2,3},{4,5},{5,6},{6,7},{8,9},{9,10},{10,11},{12,13},{... | collective-permute-start | bytes 491528 | tf_op jit(solution)/shard_map/ppermute | solution.py:17
  32.7 1.3 collective-permute-done.4
  34.3 0.6 collective-permute-done.5
  35.1 1.0 fusion.42
  36.1 0.4 fusion.106
  36.5 0.2 fusion.107
  36.7 1.9 collective-permute-start.6
  38.7 4.4 %collective-permute-start.7 = (f32[2,16,1,1280]{3,1,2,0:T(8,128)S(1)}, f32[2,16,1,1280]{3,1,2,0:T(8,128)S(1)}, u32[]{:S(2)}, u32[]{:S(2)}) collective-permute-start(f32[2,16,1,1280]{3,1,2,0:T(8,128)S(1)} %copy.34), channel_id=1, source_target_pairs={{0,1},{1,2},{2,3},{4,5},{5,6},{6,7},{8,9},{9,10},{10,11},{12,13},{... | collective-permute-start | bytes 491528 | tf_op jit(solution)/shard_map/ppermute | solution.py:17
  43.2 1.3 collective-permute-done.6
  44.7 0.6 collective-permute-done.7
  45.5 1.0 fusion.36
  46.5 0.4 fusion.103
  47.2 1.9 collective-permute-start.8
  49.1 4.6 %collective-permute-start.9 = (f32[2,16,1,1280]{3,1,2,0:T(8,128)S(1)}, f32[2,16,1,1280]{3,1,2,0:T(8,128)S(1)}, u32[]{:S(2)}, u32[]{:S(2)}) collective-permute-start(f32[2,16,1,1280]{3,1,2,0:T(8,128)S(1)} %copy.38), channel_id=1, source_target_pairs={{0,1},{1,2},{2,3},{4,5},{5,6},{6,7},{8,9},{9,10},{10,11},{12,13},{... | collective-permute-start | bytes 491528 | tf_op jit(solution)/shard_map/ppermute | solution.py:17
  53.8 1.2 collective-permute-done.8
  55.2 0.6 collective-permute-done.9
  56.0 1.1 fusion.30
  57.0 0.7 copy-done.1
  57.7 0.6 fusion
  58.3 1.3 collective-permute-start.10
  59.6 62.9 %collective-permute-done.10 = f32[4,16,8,1280]{3,2,1,0:T(8,128)S(1)} collective-permute-done((f32[4,16,8,1280]{3,2,1,0:T(8,128)S(1)}, f32[4,16,8,1280]{3,2,1,0:T(8,128)S(1)}, u32[]{:S(2)}, u32[]{:S(2)}) %collective-permute-start.10) | collective-permute-done | bytes 2621472 | tf_op jit(solution)/shard_map/ppermute | solution.py:64
  122.5 1.9 add.143
  124.4 1.2 collective-permute-start.11
  125.6 89.3 %collective-permute-done.11 = f32[4,16,8,1280]{3,2,1,0:T(8,128)} collective-permute-done((f32[4,16,8,1280]{3,2,1,0:T(8,128)}, f32[4,16,8,1280]{3,2,1,0:T(8,128)}, u32[]{:S(2)}, u32[]{:S(2)}) %collective-permute-start.11) | collective-permute-done | bytes 2621472 | tf_op jit(solution)/shard_map/ppermute | solution.py:64
  214.9 4.4 %add.144 = f32[4,16,8,1280]{3,2,1,0:T(8,128)} add(f32[4,16,8,1280]{3,2,1,0:T(8,128)} %add.143, f32[4,16,8,1280]{3,2,1,0:T(8,128)} %collective-permute-done.11) | non-fusion elementwise | flops 655360 | bytes 7864320 | tf_op jit(solution)/shard_map/add | solution.py:64
  219.4 2.1 collective-permute-start.12
  221.5 113.1 %collective-permute-done.12 = f32[4,16,8,1280]{3,2,1,0:T(8,128)} collective-permute-done((f32[4,16,8,1280]{3,2,1,0:T(8,128)}, f32[4,16,8,1280]{3,2,1,0:T(8,128)}, u32[]{:S(2)}, u32[]{:S(2)}) %collective-permute-start.12) | collective-permute-done | bytes 2621472 | tf_op jit(solution)/shard_map/ppermute | solution.py:64
  334.6 4.8 %subtract_multiply_fusion = f32[4,16,8,1280]{3,2,1,0:T(8,128)S(1)} fusion(f32[4,16,8,1280]{3,2,1,0:T(8,128)} %all-gather.3.cloned.1.call-done, f32[4,16,8,1280]{3,2,1,0:T(8,128)} %all-gather.5.cloned.1.call-done, f32[4,16,8,1280]{3,2,1,0:T(8,128)} %add.144, f32[4,16,8,1280]{3,2,1,0:T(8,128)} %collective-permute-done.12), kind=kLoop, calls=%fused_computation.4 | loop fusion | flops 1966080 | bytes 13107200 | tf_op jit(solution)/shard_map/mul | solution.py:69
  339.5 0.6 fusion.1
  340.2 0.4 fusion.100
  340.8 3.3 collective-permute-start.13
  344.2 2.2 collective-permute-start.14
  346.4 0.8 constant_dynamic-slice_fusion
  347.6 1.0 collective-permute-done.14
  348.8 1.0 fusion.23
  349.9 0.4 fusion.97
  350.5 1.9 collective-permute-start.15
  352.5 4.4 %collective-permute-start.16 = (f32[2,16,1,1280]{3,1,2,0:T(8,128)S(1)}, f32[2,16,1,1280]{3,1,2,0:T(8,128)S(1)}, u32[]{:S(2)}, u32[]{:S(2)}) collective-permute-start(f32[2,16,1,1280]{3,1,2,0:T(8,128)S(1)} %copy.46), channel_id=1, source_target_pairs={{0,1},{1,2},{2,3},{4,5},{5,6},{6,7},{8,9},{9,10},{10,11},{12,13},{... | collective-permute-start | bytes 491528 | tf_op jit(solution)/shard_map/ppermute | solution.py:17
  357.0 0.9 collective-permute-done.15
  358.1 1.0 collective-permute-done.16
  359.3 1.0 fusion.17
  360.3 0.4 fusion.94
  360.9 1.9 collective-permute-start.17
  362.9 4.6 %collective-permute-start.18 = (f32[2,16,1,1280]{3,1,2,0:T(8,128)S(1)}, f32[2,16,1,1280]{3,1,2,0:T(8,128)S(1)}, u32[]{:S(2)}, u32[]{:S(2)}) collective-permute-start(f32[2,16,1,1280]{3,1,2,0:T(8,128)S(1)} %copy.50), channel_id=1, source_target_pairs={{0,1},{1,2},{2,3},{4,5},{5,6},{6,7},{8,9},{9,10},{10,11},{12,13},{... | collective-permute-start | bytes 491528 | tf_op jit(solution)/shard_map/ppermute | solution.py:17
  367.6 0.7 collective-permute-done.17
  368.5 1.0 collective-permute-done.18
  369.7 1.1 fusion.11
  370.8 0.4 fusion.91
  371.4 1.9 collective-permute-start.19
  373.4 4.4 %collective-permute-start.20 = (f32[2,16,1,1280]{3,1,2,0:T(8,128)S(1)}, f32[2,16,1,1280]{3,1,2,0:T(8,128)S(1)}, u32[]{:S(2)}, u32[]{:S(2)}) collective-permute-start(f32[2,16,1,1280]{3,1,2,0:T(8,128)S(1)} %copy.54), channel_id=1, source_target_pairs={{0,1},{1,2},{2,3},{4,5},{5,6},{6,7},{8,9},{9,10},{10,11},{12,13},{... | collective-permute-start | bytes 491528 | tf_op jit(solution)/shard_map/ppermute | solution.py:17
  377.9 0.9 collective-permute-done.19
  379.0 1.0 collective-permute-done.20
  380.2 2.2 fusion.5
  (71 shorter events, 5.7 us)
Async XLA Ops:
  7.2 15.1 %copy-start = (f32[2,16,8,1280]{3,2,1,0:T(8,128)S(1)}, f32[2,16,8,1280]{3,2,1,0:T(8,128)}, u32[]{:S(2)}) copy-start(f32[2,16,8,1280]{3,2,1,0:T(8,128)} %param.6) | copy-start | bytes 3932164
  7.2 214.3 %all-gather.3.cloned.1.call-start = ((), (), s32[]{:S(2)}) async-start(), calls=%async_computation | async-start | bytes 2949120 | tf_op jit(solution)/shard_map/all_gather | solution.py:66
  8.1 14.9 %collective-permute-start = (f32[5,1280]{1,0:T(8,128)S(1)}, f32[5,1280]{1,0:T(8,128)S(1)}, u32[]{:S(2)}, u32[]{:S(2)}) collective-permute-start(f32[5,1280]{1,0:T(8,128)S(1)} %get-tuple-element.61), channel_id=1, source_target_pairs={{0,1},{1,2},{2,3},{4,5},{5,6},{6,7},{8,9},{9,10},{10,11},{12,13},{... | collective-permute-start | bytes 76808 | tf_op jit(solution)/shard_map/ppermute | solution.py:17
  12.6 10.4 %collective-permute-start.1 = (f32[5,1280]{1,0:T(8,128)S(1)}, f32[5,1280]{1,0:T(8,128)S(1)}, u32[]{:S(2)}, u32[]{:S(2)}) collective-permute-start(f32[5,1280]{1,0:T(8,128)S(1)} %get-tuple-element.62), channel_id=1, source_target_pairs={{1,0},{2,1},{3,2},{5,4},{6,5},{7,6},{9,8},{10,9},{11,10},{13,12},{... | collective-permute-start | bytes 76808 | tf_op jit(solution)/shard_map/ppermute | solution.py:19
  16.6 6.7 %collective-permute-start.2 = (f32[2,16,1,1280]{3,1,2,0:T(8,128)S(1)}, f32[2,16,1,1280]{3,1,2,0:T(8,128)S(1)}, u32[]{:S(2)}, u32[]{:S(2)}) collective-permute-start(f32[2,16,1,1280]{3,1,2,0:T(8,128)S(1)} %copy.56), channel_id=1, source_target_pairs={{1,0},{2,1},{3,2},{5,4},{6,5},{7,6},{9,8},{10,9},{11,10},{13,12},{... | collective-permute-start | bytes 491528 | tf_op jit(solution)/shard_map/ppermute | solution.py:19
  18.6 5.9 %collective-permute-start.3 = (f32[2,16,1,1280]{3,1,2,0:T(8,128)S(1)}, f32[2,16,1,1280]{3,1,2,0:T(8,128)S(1)}, u32[]{:S(2)}, u32[]{:S(2)}) collective-permute-start(f32[2,16,1,1280]{3,1,2,0:T(8,128)S(1)} %copy.57), channel_id=1, source_target_pairs={{0,1},{1,2},{2,3},{4,5},{5,6},{6,7},{8,9},{9,10},{10,11},{12,13},{... | collective-permute-start | bytes 491528 | tf_op jit(solution)/shard_map/ppermute | solution.py:17
  22.2 0.8 copy-start.4
  22.2 0.8 copy-start.3
  22.3 199.2 %all-gather.5.cloned.1.call-start = ((), (), s32[]{:S(2)}) async-start(), calls=%async_computation.1 | async-start | bytes 2949120 | tf_op jit(solution)/shard_map/all_gather | solution.py:67
  26.3 7.8 %collective-permute-start.4 = (f32[2,16,1,1280]{3,1,2,0:T(8,128)S(1)}, f32[2,16,1,1280]{3,1,2,0:T(8,128)S(1)}, u32[]{:S(2)}, u32[]{:S(2)}) collective-permute-start(f32[2,16,1,1280]{3,1,2,0:T(8,128)S(1)} %copy.28), channel_id=1, source_target_pairs={{1,0},{2,1},{3,2},{5,4},{6,5},{7,6},{9,8},{10,9},{11,10},{13,12},{... | collective-permute-start | bytes 491528 | tf_op jit(solution)/shard_map/ppermute | solution.py:19
  28.3 6.6 %collective-permute-start.5 = (f32[2,16,1,1280]{3,1,2,0:T(8,128)S(1)}, f32[2,16,1,1280]{3,1,2,0:T(8,128)S(1)}, u32[]{:S(2)}, u32[]{:S(2)}) collective-permute-start(f32[2,16,1,1280]{3,1,2,0:T(8,128)S(1)} %copy.30), channel_id=1, source_target_pairs={{0,1},{1,2},{2,3},{4,5},{5,6},{6,7},{8,9},{9,10},{10,11},{12,13},{... | collective-permute-start | bytes 491528 | tf_op jit(solution)/shard_map/ppermute | solution.py:17
  36.7 7.8 %collective-permute-start.6 = (f32[2,16,1,1280]{3,1,2,0:T(8,128)S(1)}, f32[2,16,1,1280]{3,1,2,0:T(8,128)S(1)}, u32[]{:S(2)}, u32[]{:S(2)}) collective-permute-start(f32[2,16,1,1280]{3,1,2,0:T(8,128)S(1)} %copy.32), channel_id=1, source_target_pairs={{1,0},{2,1},{3,2},{5,4},{6,5},{7,6},{9,8},{10,9},{11,10},{13,12},{... | collective-permute-start | bytes 491528 | tf_op jit(solution)/shard_map/ppermute | solution.py:19
  38.7 6.6 %collective-permute-start.7 = (f32[2,16,1,1280]{3,1,2,0:T(8,128)S(1)}, f32[2,16,1,1280]{3,1,2,0:T(8,128)S(1)}, u32[]{:S(2)}, u32[]{:S(2)}) collective-permute-start(f32[2,16,1,1280]{3,1,2,0:T(8,128)S(1)} %copy.34), channel_id=1, source_target_pairs={{0,1},{1,2},{2,3},{4,5},{5,6},{6,7},{8,9},{9,10},{10,11},{12,13},{... | collective-permute-start | bytes 491528 | tf_op jit(solution)/shard_map/ppermute | solution.py:17
  47.2 7.8 %collective-permute-start.8 = (f32[2,16,1,1280]{3,1,2,0:T(8,128)S(1)}, f32[2,16,1,1280]{3,1,2,0:T(8,128)S(1)}, u32[]{:S(2)}, u32[]{:S(2)}) collective-permute-start(f32[2,16,1,1280]{3,1,2,0:T(8,128)S(1)} %copy.36), channel_id=1, source_target_pairs={{1,0},{2,1},{3,2},{5,4},{6,5},{7,6},{9,8},{10,9},{11,10},{13,12},{... | collective-permute-start | bytes 491528 | tf_op jit(solution)/shard_map/ppermute | solution.py:19
  49.1 6.6 %collective-permute-start.9 = (f32[2,16,1,1280]{3,1,2,0:T(8,128)S(1)}, f32[2,16,1,1280]{3,1,2,0:T(8,128)S(1)}, u32[]{:S(2)}, u32[]{:S(2)}) collective-permute-start(f32[2,16,1,1280]{3,1,2,0:T(8,128)S(1)} %copy.38), channel_id=1, source_target_pairs={{0,1},{1,2},{2,3},{4,5},{5,6},{6,7},{8,9},{9,10},{10,11},{12,13},{... | collective-permute-start | bytes 491528 | tf_op jit(solution)/shard_map/ppermute | solution.py:17
  56.0 1.8 copy-start.1
  58.3 64.2 %collective-permute-start.10 = (f32[4,16,8,1280]{3,2,1,0:T(8,128)S(1)}, f32[4,16,8,1280]{3,2,1,0:T(8,128)S(1)}, u32[]{:S(2)}, u32[]{:S(2)}) collective-permute-start(f32[4,16,8,1280]{3,2,1,0:T(8,128)S(1)} %fusion), channel_id=1, source_target_pairs={{0,4},{4,0},{8,12},{12,8},{16,20},{20,16},{24,28},{28,24},{1,5},{5... | collective-permute-start | bytes 7864328 | tf_op jit(solution)/shard_map/ppermute | solution.py:64
  124.4 90.5 %collective-permute-start.11 = (f32[4,16,8,1280]{3,2,1,0:T(8,128)}, f32[4,16,8,1280]{3,2,1,0:T(8,128)}, u32[]{:S(2)}, u32[]{:S(2)}) collective-permute-start(f32[4,16,8,1280]{3,2,1,0:T(8,128)} %add.143), channel_id=1, source_target_pairs={{0,8},{4,12},{8,0},{12,4},{16,24},{20,28},{24,16},{28,20},{1,9},{5... | collective-permute-start | bytes 7864328 | tf_op jit(solution)/shard_map/ppermute | solution.py:64
  219.4 115.3 %collective-permute-start.12 = (f32[4,16,8,1280]{3,2,1,0:T(8,128)}, f32[4,16,8,1280]{3,2,1,0:T(8,128)}, u32[]{:S(2)}, u32[]{:S(2)}) collective-permute-start(f32[4,16,8,1280]{3,2,1,0:T(8,128)} %add.144), channel_id=1, source_target_pairs={{0,16},{4,20},{8,24},{12,28},{16,0},{20,4},{24,8},{28,12},{1,17},{... | collective-permute-start | bytes 7864328 | tf_op jit(solution)/shard_map/ppermute | solution.py:64
  334.6 4.8 %copy-start.2 = (bf16[4,2,16,8,1280]{4,3,2,1,0:T(8,128)(2,1)S(1)}, bf16[4,2,16,8,1280]{4,3,2,1,0:T(8,128)(2,1)}, u32[]{:S(2)}) copy-start(bf16[4,2,16,8,1280]{4,3,2,1,0:T(8,128)(2,1)} %param.7) | copy-start | bytes 7864324
  340.8 6.6 %collective-permute-start.13 = (f32[2,16,1,1280]{3,1,2,0:T(8,128)S(1)}, f32[2,16,1,1280]{3,1,2,0:T(8,128)S(1)}, u32[]{:S(2)}, u32[]{:S(2)}) collective-permute-start(f32[2,16,1,1280]{3,1,2,0:T(8,128)S(1)} %copy.40), channel_id=1, source_target_pairs={{1,0},{2,1},{3,2},{5,4},{6,5},{7,6},{9,8},{10,9},{11,10},{13,12},{... | collective-permute-start | bytes 491528 | tf_op jit(solution)/shard_map/ppermute | solution.py:19
  344.2 4.5 %collective-permute-start.14 = (f32[2,16,1,1280]{3,1,2,0:T(8,128)S(1)}, f32[2,16,1,1280]{3,1,2,0:T(8,128)S(1)}, u32[]{:S(2)}, u32[]{:S(2)}) collective-permute-start(f32[2,16,1,1280]{3,1,2,0:T(8,128)S(1)} %copy.42), channel_id=1, source_target_pairs={{0,1},{1,2},{2,3},{4,5},{5,6},{6,7},{8,9},{9,10},{10,11},{12,13},{... | collective-permute-start | bytes 491528 | tf_op jit(solution)/shard_map/ppermute | solution.py:17
  350.5 7.4 %collective-permute-start.15 = (f32[2,16,1,1280]{3,1,2,0:T(8,128)S(1)}, f32[2,16,1,1280]{3,1,2,0:T(8,128)S(1)}, u32[]{:S(2)}, u32[]{:S(2)}) collective-permute-start(f32[2,16,1,1280]{3,1,2,0:T(8,128)S(1)} %copy.44), channel_id=1, source_target_pairs={{1,0},{2,1},{3,2},{5,4},{6,5},{7,6},{9,8},{10,9},{11,10},{13,12},{... | collective-permute-start | bytes 491528 | tf_op jit(solution)/shard_map/ppermute | solution.py:19
  352.5 6.6 %collective-permute-start.16 = (f32[2,16,1,1280]{3,1,2,0:T(8,128)S(1)}, f32[2,16,1,1280]{3,1,2,0:T(8,128)S(1)}, u32[]{:S(2)}, u32[]{:S(2)}) collective-permute-start(f32[2,16,1,1280]{3,1,2,0:T(8,128)S(1)} %copy.46), channel_id=1, source_target_pairs={{0,1},{1,2},{2,3},{4,5},{5,6},{6,7},{8,9},{9,10},{10,11},{12,13},{... | collective-permute-start | bytes 491528 | tf_op jit(solution)/shard_map/ppermute | solution.py:17
  360.9 7.4 %collective-permute-start.17 = (f32[2,16,1,1280]{3,1,2,0:T(8,128)S(1)}, f32[2,16,1,1280]{3,1,2,0:T(8,128)S(1)}, u32[]{:S(2)}, u32[]{:S(2)}) collective-permute-start(f32[2,16,1,1280]{3,1,2,0:T(8,128)S(1)} %copy.48), channel_id=1, source_target_pairs={{1,0},{2,1},{3,2},{5,4},{6,5},{7,6},{9,8},{10,9},{11,10},{13,12},{... | collective-permute-start | bytes 491528 | tf_op jit(solution)/shard_map/ppermute | solution.py:19
  362.9 6.6 %collective-permute-start.18 = (f32[2,16,1,1280]{3,1,2,0:T(8,128)S(1)}, f32[2,16,1,1280]{3,1,2,0:T(8,128)S(1)}, u32[]{:S(2)}, u32[]{:S(2)}) collective-permute-start(f32[2,16,1,1280]{3,1,2,0:T(8,128)S(1)} %copy.50), channel_id=1, source_target_pairs={{0,1},{1,2},{2,3},{4,5},{5,6},{6,7},{8,9},{9,10},{10,11},{12,13},{... | collective-permute-start | bytes 491528 | tf_op jit(solution)/shard_map/ppermute | solution.py:17
  371.4 7.4 %collective-permute-start.19 = (f32[2,16,1,1280]{3,1,2,0:T(8,128)S(1)}, f32[2,16,1,1280]{3,1,2,0:T(8,128)S(1)}, u32[]{:S(2)}, u32[]{:S(2)}) collective-permute-start(f32[2,16,1,1280]{3,1,2,0:T(8,128)S(1)} %copy.52), channel_id=1, source_target_pairs={{1,0},{2,1},{3,2},{5,4},{6,5},{7,6},{9,8},{10,9},{11,10},{13,12},{... | collective-permute-start | bytes 491528 | tf_op jit(solution)/shard_map/ppermute | solution.py:19
  373.4 6.6 %collective-permute-start.20 = (f32[2,16,1,1280]{3,1,2,0:T(8,128)S(1)}, f32[2,16,1,1280]{3,1,2,0:T(8,128)S(1)}, u32[]{:S(2)}, u32[]{:S(2)}) collective-permute-start(f32[2,16,1,1280]{3,1,2,0:T(8,128)S(1)} %copy.54), channel_id=1, source_target_pairs={{0,1},{1,2},{2,3},{4,5},{5,6},{6,7},{8,9},{9,10},{10,11},{12,13},{... | collective-permute-start | bytes 491528 | tf_op jit(solution)/shard_map/ppermute | solution.py:17
Sparse Core Ops, SparseCore 0:
  22.4 58.7 all-gather.2
  125.8 79.4 all-gather.4
